TPU v7x, 1024 devices: a whole 4x4x32 slice. The times are simulated.
1024 devices in a mesh: dp: 64 (over y, z_lo, core), tensor: 16 (over x, z_hi).
Axes of the slice: x: 4, y: 4, z: 32 (z_hi: 4, z_lo: 8; z = z_hi * 8 + z_lo), core: 2. Of those that a mesh axis runs over, the one named last changes fastest.
Arguments:
- inputs: bfloat16 [128, 9216], P('tensor', 'dp'), may hold values from -6 to 6
- grad_out: bfloat16 [128, 9216], P('tensor', 'dp'), may hold values from -3 to 3
- saved_pre: bfloat16 [128, 36864], P('dp', 'tensor'), may hold values from -8 to 8
- w_in: bfloat16 [9216, 36864], P('dp', 'tensor'), may hold values from -0.0625 to 0.0625
- w_out: bfloat16 [36864, 9216], P('tensor', 'dp'), may hold values from -0.03125 to 0.03125
Outputs:
- grad_in: bfloat16 [128, 9216], P('tensor', 'dp')
- grad_w_in: bfloat16 [9216, 36864], P('dp', 'tensor')
- grad_w_out: bfloat16 [36864, 9216], P('tensor', 'dp')
All inputs are finite; a program needn't handle non-finite values.
Results may differ from a plain program's by a relative error of at most 0.015.
Values may be sent and summed in bfloat16 or wider, within the bound.
A program may use at most 32 MiB of HBM per device.

v0:
```python
import jax
import jax.numpy as jnp
from jax import lax
from jax.sharding import PartitionSpec as P

root_half = 0.7071067811865476
inv_root_two_pi = 0.3989422804014327


def gelu_parts(saved):
    value = saved.astype(jnp.float32)
    cdf = 0.5 * (1.0 + lax.erf(value * root_half))
    density = inv_root_two_pi * jnp.exp(-0.5 * value * value)
    return (value * cdf, cdf + value * density)


def on_device(inputs, grad_out, saved_pre, w_in, w_out):
    grad_rows, input_rows = (
        lax.all_gather(grad_out, "tensor", axis=0, tiled=True),
        lax.all_gather(inputs, "tensor", axis=0, tiled=True),
    )
    block = grad_rows
    grad_hidden = lax.psum_scatter(
        lax.dot_general(block, w_out, (((1,), (1,)), ((), ())), preferred_element_type=jnp.float32),
        "dp",
        scatter_dimension=0,
        tiled=True,
    )
    activated, slope = gelu_parts(saved_pre)
    grad_pre = (grad_hidden * slope).astype(jnp.bfloat16)
    grad_all, hidden_all = (
        lax.all_gather(grad_pre, "dp", axis=0, tiled=True),
        lax.all_gather(activated.astype(jnp.bfloat16), "dp", axis=0, tiled=True),
    )
    block = grad_all
    grad_in = lax.psum_scatter(
        lax.dot_general(
            block, w_in, (((1,), (1,)), ((), ())), preferred_element_type=jnp.float32
        ).astype(jnp.bfloat16),
        "tensor",
        scatter_dimension=0,
        tiled=True,
    )
    grad_w_in = lax.dot_general(
        input_rows, grad_all, (((0,), (0,)), ((), ())), preferred_element_type=jnp.float32
    ).astype(jnp.bfloat16)
    grad_w_out = lax.dot_general(
        hidden_all, grad_rows, (((0,), (0,)), ((), ())), preferred_element_type=jnp.float32
    ).astype(jnp.bfloat16)
    return (grad_in, grad_w_in, grad_w_out)


def solution(mesh):
    return jax.shard_map(
        on_device,
        mesh=mesh,
        in_specs=(
            P("tensor", "dp"),
            P("tensor", "dp"),
            P("dp", "tensor"),
            P("dp", "tensor"),
            P("tensor", "dp"),
        ),
        out_specs=(P("tensor", "dp"), P("dp", "tensor"), P("tensor", "dp")),
        check_vma=False,
    )
```

profile of v0, /device:TPU:1, one launch (start us, length us, event | category | flops | bytes accessed | tf_op | source)
XLA Modules:
  0.0 1211.6 jit_solution(4570535085630521647)
XLA Ops:
  7.2 0.0 copy-start
  7.2 0.0 all-reduce.3.cloned.1.call-start
  7.2 82.0 %all_gather.12 = bf16[128,144]{1,0:T(8,128)(2,1)S(1)} all-gather(bf16[8,144]{1,0:T(8,128)(2,1)} %param.6), channel_id=1, replica_groups=mesh['dp'=64,'tensor'=16] {'tensor'}, dimensions={0}, use_global_device_ids=true | all-gather | bytes 39168 | tf_op jit(solution)/shard_map/all_gather | solution.py:19
  89.3 0.0 copy-done
  89.3 0.0 copy-start.2
  89.3 1.3 fusion.13
  90.6 0.0 all-reduce.3.cloned.1.call-update
  90.6 0.0 copy-start.3
  90.6 0.0 reduce-scatter.2.cloned.1.call-start
  90.7 0.0 copy-done.2
  90.7 128.6 %all-gather.1 = bf16[64,2,2304]{2,1,0:T(2,128)(2,1)S(1)} all-gather(bf16[1,2,2304]{2,1,0:T(2,128)(2,1)S(1)} %get-tuple-element.3), channel_id=1, replica_groups=mesh['dp'=64,'tensor'=16] {'dp'}, dimensions={0}, use_global_device_ids=true | all-gather | bytes 599040 | tf_op jit(solution)/shard_map/all_gather | solution.py:33
  219.3 0.2 reshape.9
  219.5 1.3 dynamic-slice
  221.5 0.0 copy-done.3
  221.5 62.1 %all_gather.14 = bf16[128,144]{1,0:T(8,128)(2,1)S(1)} all-gather(bf16[8,144]{1,0:T(8,128)(2,1)S(1)} %copy-done.3), channel_id=1, replica_groups=mesh['dp'=64,'tensor'=16] {'tensor'}, dimensions={0}, use_global_device_ids=true | all-gather | bytes 39168 | tf_op jit(solution)/shard_map/all_gather | solution.py:20
  283.6 1.2 convolution_convert_fusion
  284.8 0.0 copy-start.1
  284.8 632.2 %all-reduce.3.cloned.1.call-done = f32[128,2304]{1,0:T(8,128)} async-done(((f32[128,2304]{1,0:T(8,128)}), f32[128,2304]{1,0:T(8,128)}) %all-reduce.3.cloned.1.call-update) | async-done | bytes 1179664
  917.0 0.9 fusion.11
  917.9 122.4 %all-gather = bf16[64,2,2304]{2,1,0:T(2,128)(2,1)S(1)} all-gather(bf16[1,2,2304]{2,1,0:T(2,128)(2,1)S(1)} %fusion.11), channel_id=1, replica_groups=mesh['dp'=64,'tensor'=16] {'dp'}, dimensions={0}, use_global_device_ids=true | all-gather | bytes 599040 | tf_op jit(solution)/shard_map/all_gather | solution.py:32
  1040.4 0.2 reshape.7
  1040.6 0.0 copy-done.1
  1040.6 1.0 convolution_convert_fusion.2
  1041.5 0.0 reduce-scatter.2.cloned.1.call-update
  1041.6 1.2 fusion
  1042.8 162.0 %reduce-scatter.2.cloned.1.call-done = bf16[8,144]{1,0:T(8,128)(2,1)} async-done(((bf16[128,144]{1,0:T(8,128)(2,1)}), bf16[8,144]{1,0:T(8,128)(2,1)}) %reduce-scatter.2.cloned.1.call-update) | async-done | bytes 2320 | tf_op jit(solution)/shard_map/reduce_scatter | solution.py:36
  (1 shorter events, 0.0 us)
Async XLA Ops:
  7.2 82.1 %copy-start = (bf16[2304,144]{0,1:T(8,128)(2,1)S(1)}, bf16[2304,144]{0,1:T(8,128)(2,1)}, u32[]{:S(2)}) copy-start(bf16[2304,144]{0,1:T(8,128)(2,1)} %param.9) | copy-start | bytes 1990660
  7.2 909.8 %all-reduce.3.cloned.1.call-start = ((), (), s32[]{:S(2)}) async-start(), calls=%async_computation.2 | async-start | bytes 2359296
  89.3 1.4 copy-start.2
  90.6 130.8 %copy-start.3 = (bf16[8,144]{1,0:T(8,128)(2,1)S(1)}, bf16[8,144]{1,0:T(8,128)(2,1)}, u32[]{:S(2)}) copy-start(bf16[8,144]{1,0:T(8,128)(2,1)} %param.5) | copy-start | bytes 6916
  90.6 1114.1 %reduce-scatter.2.cloned.1.call-start = ((), (), s32[]{:S(2)}) async-start(), calls=%async_computation.1 | async-start | bytes 69632 | tf_op jit(solution)/shard_map/reduce_scatter | solution.py:36
  284.8 755.8 %copy-start.1 = (bf16[144,2304]{1,0:T(8,128)(2,1)S(1)}, bf16[144,2304]{1,0:T(8,128)(2,1)}, u32[]{:S(2)}) copy-start(bf16[144,2304]{1,0:T(8,128)(2,1)} %param.8) | copy-start | bytes 1990660
Sparse Core Ops, SparseCore 0:
  90.7 826.1 all-reduce.2
  1041.7 163.0 reduce-scatter.1
where the time goes:
time: 1210 us
  waiting for transfers between devices  794 us (66%)
  blocking collectives  395 us (33%)
  between operations  14.8 us (1%)
    unnamed x3, waiting for transfers between devices  632 us
    reduce_scatter x1, waiting for transfers between devices, on_device(): lax.psum_scatter(lax.dot_general(block, w_in, (((1,), (1,)), ((), ())), p...  162 us
    all_gather x1, blocking collectives, on_device(): lax.all_gather(activated.astype(jnp.bfloat16), 'dp', axis=0, tiled=True)  129 us
    all_gather x1, blocking collectives, on_device(): lax.all_gather(grad_pre, 'dp', axis=0, tiled=True)  122 us
    all_gather x1, blocking collectives, on_device(): lax.all_gather(grad_out, 'tensor', axis=0, tiled=True)  82 us
    all_gather x1, blocking collectives, on_device(): lax.all_gather(inputs, 'tensor', axis=0, tiled=True)  62.1 us
  transfers between devices with their start and end apart: 2, of which 2 were waited for; matrix products, arithmetic and copies ran while one was open for 0% of the time, Pallas kernels for 0%

commit v1 on v0

v1 whole, which is shorter than its diff:
```python
import functools

import jax
import jax.numpy as jnp
from jax import lax
from jax.experimental import pallas as pl
from jax.experimental.pallas import tpu as pltpu
from jax.sharding import PartitionSpec as P

GRID = dict(ny=4, nz=8, nx=4, nh=4)

root_half = 0.7071067811865476
inv_root_two_pi = 0.3989422804014327
bf16, f32 = jnp.bfloat16, jnp.float32


def gelu_parts(saved):
    value = saved.astype(f32)
    cdf = 0.5 * (1.0 + lax.erf(value * root_half))
    density = inv_root_two_pi * jnp.exp(-0.5 * value * value)
    return value * cdf, cdf + value * density


def kernel(
    ny, nz, nx, nh,
    x_hbm, g_hbm, s_hbm, wi_hbm, wo_hbm,
    gin_hbm, gwi_hbm, gwo_hbm,
    rows, own_s, peer_s, wi_v, wo_v, wide, grad_rows, input_rows,
    slope, quad, hid, pre,
    b1_send, b1_recv, b1_own, b2_send, b2_recv, b2_sum, b3_send, b3_own, b3_recv,
    pack, hid_full, pre_full, gwi_v, gwo_v,
    dx_part, dx_send, dx_recv, dz_part, dz_send, dz_recv, gin_v,
    local_sem, send_sem,
    az_sem, ax_sem, s_sem, hz_sem, hy_sem, hc_sem,
    b1_sem, b2_sem, b3_sem, c1_sem, c2_sem, c3_sem, dx_sem, dz_sem,
):
    dp, tp = lax.axis_index("dp"), lax.axis_index("tensor")
    core = lax.rem(dp, 2)
    chip = lax.div(dp, 2)
    z, y = lax.rem(chip, nz), lax.div(chip, nz)
    x, h = lax.div(tp, nh), lax.rem(tp, nh)
    other = 1 - core

    def at(y=y, z=z, core=core, x=x, h=h):
        return {"dp": (y * nz + z) * 2 + core, "tensor": x * nh + h}

    y_peer = [None] + [at(y=lax.rem(y + k, ny)) for k in range(1, ny)]
    z_peer = [None] + [at(z=lax.rem(z + k, nz)) for k in range(1, nz)]
    x_peer = [None] + [at(x=lax.rem(x + k, nx)) for k in range(1, nx)]
    right, left = at(h=lax.rem(h + 1, nh)), at(h=lax.rem(h + nh - 1, nh))
    partner = at(core=other)
    peers = y_peer[1:] + z_peer[1:] + x_peer[1:] + [right, left, partner]

    half = wi_v.shape[2]
    width = wi_v.shape[1]
    tokens = b1_send.shape[0] * b1_send.shape[1]

    loads = []

    def load(src, dst):
        copy = pltpu.make_async_copy(src, dst, local_sem.at[len(loads)])
        copy.start()
        loads.append(copy)
        return copy

    load_g = load(g_hbm, rows.at[tp, 0])
    load_x = load(x_hbm, rows.at[tp, 1])
    load_s = [load(s_hbm.at[:, pl.ds(i * half, half)], own_s.at[i]) for i in range(2)]
    load_wo = [load(wo_hbm.at[:, pl.ds(i * half, half)], wo_v.at[i]) for i in range(2)]
    load_wi = [load(wi_hbm.at[:, pl.ds(i * half, half)], wi_v.at[i]) for i in range(2)]

    barrier = pltpu.get_barrier_semaphore()
    for peer in peers:
        pl.semaphore_signal(barrier, inc=1, device_id=peer, device_id_type=pl.DeviceIdType.MESH)
    pl.semaphore_wait(barrier, len(peers))

    sends = []

    def send(src, dst, recv_sem, peer):
        copy = pltpu.make_async_remote_copy(
            src_ref=src, dst_ref=dst, send_sem=send_sem.at[len(sends)], recv_sem=recv_sem,
            device_id=peer, device_id_type=pl.DeviceIdType.MESH,
        )
        copy.start()
        sends.append(copy)

    def arrived(dst, recv_sem):
        pltpu.make_async_remote_copy(
            src_ref=dst, dst_ref=dst, send_sem=send_sem.at[0], recv_sem=recv_sem,
            device_id=partner, device_id_type=pl.DeviceIdType.MESH,
        ).wait_recv()

    slot = lambda x_, h_: x_ * nh + h_
    h_left, h_right, h_far = lax.rem(h + nh - 1, nh), lax.rem(h + 1, nh), lax.rem(h + 2, nh)

    def to_x(which, h_):
        block = rows.at[slot(x, h_)]
        for k in range(1, nx):
            send(block, block, ax_sem.at[k - 1, which], x_peer[k])

    load_g.wait()
    load_x.wait()
    mine = rows.at[tp]
    send(mine, mine, az_sem.at[0], right)
    send(mine, mine, az_sem.at[1], left)

    for copy in load_s:
        copy.wait()
    send(own_s.at[other], peer_s, s_sem.at[0], partner)
    to_x(0, h)

    arrived(peer_s, s_sem.at[0])
    own, peer = gelu_parts(own_s[core]), gelu_parts(peer_s[...])
    n = own[0].shape[0]
    first = core == 0
    for ref, i in ((quad, 0), (slope, 1)):
        ref[0:n, :] = jnp.where(first, own[i], peer[i])
        ref[n : 2 * n, :] = jnp.where(first, peer[i], own[i])
    hid[core, y, z] = quad[...].astype(bf16)

    def to_z(buf, sem):
        block = buf.at[core, y, z]
        for k in range(1, nz):
            send(block, block, sem.at[k - 1], z_peer[k])

    def from_z(buf, sem):
        for k in range(1, nz):
            arrived(buf.at[core, y, lax.rem(z + nz - k, nz)], sem.at[k - 1])

    def to_y(buf, sem):
        block = buf.at[core, y]
        for k in range(1, ny):
            send(block, block, sem.at[k - 1], y_peer[k])

    def from_y(buf, sem, k):
        arrived(buf.at[core, lax.rem(y + ny - k, ny)], sem.at[k - 1])

    to_z(hid, hz_sem)

    from_left = rows.at[slot(x, h_left)]
    arrived(from_left, az_sem.at[0])
    send(from_left, from_left, az_sem.at[2], right)
    to_x(1, h_left)
    arrived(rows.at[slot(x, h_right)], az_sem.at[1])
    to_x(2, h_right)
    from_z(hid, hz_sem)
    to_y(hid, hy_sem)
    arrived(rows.at[slot(x, h_far)], az_sem.at[2])
    to_x(3, h_far)
    for copy in load_wo:
        copy.wait()
    for which, h_ in enumerate((h, h_left, h_right, h_far)):
        for k in range(1, nx):
            arrived(rows.at[slot(lax.rem(x + nx - k, nx), h_)], ax_sem.at[k - 1, which])

    def gathered(which, out):
        step = rows.shape[2]
        for t in range(rows.shape[0]):
            wide[t * step : (t + 1) * step, :] = rows[t, which].astype(f32)
        out[...] = wide[...].astype(bf16)

    gathered(0, grad_rows)

    def product(which):
        return jnp.dot(grad_rows[...], wo_v[which], preferred_element_type=f32)

    b1_send[...] = product(other).astype(bf16).reshape(b1_send.shape)
    for k in list(range(1, ny)) + [0]:
        y_ = lax.rem(y + k, ny)
        send(b1_send.at[y_], b1_recv.at[y_], b1_sem.at[k], partner)
    b1_own[...] = product(core).reshape(b1_own.shape)
    for k in range(1, ny):
        from_y(hid, hy_sem, k)
    for k in list(range(1, ny)) + [0]:
        y_ = lax.rem(y + k, ny)
        arrived(b1_recv.at[y_], b1_sem.at[k])
        total = b1_own[y_] + b1_recv[y_].astype(f32)
        if k:
            b2_send[k - 1] = total.astype(bf16)
            send(b2_send.at[k - 1], b2_recv.at[k - 1], b2_sem.at[k - 1], y_peer[k])
        else:
            b2_sum[...] = total
    send(hid.at[core], hid.at[core], hc_sem.at[0], partner)
    for k in range(1, ny):
        arrived(b2_recv.at[k - 1], b2_sem.at[k - 1])
    total = b2_sum[...]
    for k in range(1, ny):
        total = total + b2_recv[k - 1].astype(f32)
    b2_sum[...] = total
    deep = b3_own.shape[1]
    for j in range(nz):
        piece = b2_sum[j * deep : (j + 1) * deep, :]
        b3_own[j] = piece
        b3_send[j] = piece.astype(bf16)
    for k in range(1, nz):
        send(b3_send.at[lax.rem(z + k, nz)], b3_recv.at[k - 1], b3_sem.at[k - 1], z_peer[k])
    total = b3_own[z]
    for k in range(1, nz):
        arrived(b3_recv.at[k - 1], b3_sem.at[k - 1])
        total = total + b3_recv[k - 1].astype(f32)
    pre[core, y, z] = (total * slope[...]).astype(bf16)

    to_z(pre, c1_sem)
    gathered(1, input_rows)
    from_z(pre, c1_sem)
    to_y(pre, c2_sem)
    send(pre.at[core, y], pre.at[core, y], c3_sem.at[0], partner)
    for k in range(1, ny):
        from_y(pre, c2_sem, k)
        block = pre.at[core, lax.rem(y + ny - k, ny)]
        send(block, block, c3_sem.at[k], partner)

    def packed(buf, which, out):
        for i in range(ny):
            for j in range(nz):
                r = (i * nz + j) * deep
                pack[r : r + deep, :] = buf[which, i, j].astype(f32)
        out[which] = pack[...].astype(bf16)

    def back(which):
        return lax.dot_general(
            pre_full[which], wi_v[which], (((1,), (1,)), ((), ())), preferred_element_type=f32
        )

    for copy in load_wi:
        copy.wait()
    packed(pre, core, pre_full)
    part = back(core)
    for k in range(ny):
        arrived(pre.at[other, lax.rem(y + ny - k, ny)], c3_sem.at[k])
    packed(pre, other, pre_full)
    part = part + back(other)

    dx_part[...] = part.reshape(dx_part.shape)
    for k in range(1, nx):
        dx_send[k - 1] = dx_part[lax.rem(x + k, nx)].astype(bf16)
        send(dx_send.at[k - 1], dx_recv.at[k - 1], dx_sem.at[k - 1], x_peer[k])
    arrived(hid.at[other], hc_sem.at[0])
    packed(hid, 0, hid_full)
    packed(hid, 1, hid_full)
    total = dx_part[x]
    for k in range(1, nx):
        arrived(dx_recv.at[k - 1], dx_sem.at[k - 1])
        total = total + dx_recv[k - 1].astype(f32)
    dz_part[...] = total.reshape(dz_part.shape)
    dz_send[0] = dz_part[h_far].astype(bf16)
    dz_send[1] = dz_part[h_left].astype(bf16)
    send(dz_send.at[0], dz_recv.at[0], dz_sem.at[0], right)
    send(dz_send.at[1], dz_recv.at[1], dz_sem.at[1], left)

    def outer(a, b):
        return lax.dot_general(
            a[...], b, (((0,), (0,)), ((), ())), preferred_element_type=f32
        ).astype(bf16)

    for i in range(2):
        gwi_v[:, i * half : (i + 1) * half] = outer(input_rows, pre_full[i])
    out_wi = load(gwi_v, gwi_hbm)
    arrived(dz_recv.at[0], dz_sem.at[0])
    dz_send[2] = (dz_part[h_right] + dz_recv[0].astype(f32)).astype(bf16)
    send(dz_send.at[2], dz_recv.at[2], dz_sem.at[2], right)
    for i in range(2):
        gwo_v[:, i * half : (i + 1) * half] = outer(grad_rows, hid_full[i])
    out_wo = load(gwo_v, gwo_hbm)
    arrived(dz_recv.at[1], dz_sem.at[1])
    arrived(dz_recv.at[2], dz_sem.at[2])
    gin_v[...] = (dz_part[h] + dz_recv[1].astype(f32) + dz_recv[2].astype(f32)).astype(bf16)
    out_in = load(gin_v, gin_hbm)
    for copy in sends:
        copy.wait_send()
    for copy in (out_wi, out_wo, out_in):
        copy.wait()


def on_device(inputs, grad_out, saved_pre, w_in, w_out):
    ny, nz, nx, nh = (GRID[k] for k in ("ny", "nz", "nx", "nh"))
    step, width = inputs.shape
    n, hidden = saved_pre.shape
    half = hidden // 2
    tokens = step * nx * nh
    deep = tokens // (ny * nz)
    per_y, per_x = tokens // ny, tokens // nx
    vmem, dma = pltpu.VMEM, pltpu.SemaphoreType.DMA
    any_space = pl.BlockSpec(memory_space=pl.ANY)
    n_sends = 3 + 4 * (nx - 1) + 1 + 3 * (nz - 1) + 3 * (ny - 1) + ny + 1 + ny + (nx - 1) + 3
    grad_in, grad_w_in, grad_w_out = pl.pallas_call(
        functools.partial(kernel, ny, nz, nx, nh),
        out_shape=(
            jax.ShapeDtypeStruct((step, width), bf16),
            jax.ShapeDtypeStruct((width, hidden), bf16),
            jax.ShapeDtypeStruct((width, hidden), bf16),
        ),
        in_specs=[any_space] * 5,
        out_specs=(any_space,) * 3,
        scratch_shapes=[
            vmem((nx * nh, 2, step, width), bf16),
            vmem((2, n, half), bf16),
            vmem((n, half), bf16),
            vmem((2, width, half), bf16),
            vmem((2, width, half), bf16),
            vmem((tokens, width), f32),
            vmem((tokens, width), bf16),
            vmem((tokens, width), bf16),
            vmem((deep, half), f32),
            vmem((deep, half), f32),
            vmem((2, ny, nz, deep, half), bf16),
            vmem((2, ny, nz, deep, half), bf16),
            vmem((ny, per_y, half), bf16),
            vmem((ny, per_y, half), bf16),
            vmem((ny, per_y, half), f32),
            vmem((ny - 1, per_y, half), bf16),
            vmem((ny - 1, per_y, half), bf16),
            vmem((per_y, half), f32),
            vmem((nz, deep, half), bf16),
            vmem((nz, deep, half), f32),
            vmem((nz - 1, deep, half), bf16),
            vmem((tokens, half), f32),
            vmem((2, tokens, half), bf16),
            vmem((2, tokens, half), bf16),
            vmem((width, hidden), bf16),
            vmem((width, hidden), bf16),
            vmem((nx, per_x, width), f32),
            vmem((nx - 1, per_x, width), bf16),
            vmem((nx - 1, per_x, width), bf16),
            vmem((nh, step, width), f32),
            vmem((3, step, width), bf16),
            vmem((3, step, width), bf16),
            vmem((step, width), bf16),
            dma((11,)),
            dma((n_sends,)),
            dma((3,)),
            dma((nx - 1, 4)),
            dma((1,)),
            dma((nz - 1,)),
            dma((ny - 1,)),
            dma((1,)),
            dma((ny,)),
            dma((ny - 1,)),
            dma((nz - 1,)),
            dma((nz - 1,)),
            dma((ny - 1,)),
            dma((ny,)),
            dma((nx - 1,)),
            dma((3,)),
        ],
        compiler_params=pltpu.CompilerParams(
            collective_id=0, has_side_effects=True, vmem_limit_bytes=48 * 1024 * 1024
        ),
    )(inputs, grad_out, saved_pre, w_in, w_out.T)
    return grad_in, grad_w_in, grad_w_out.T


def solution(mesh):
    return jax.shard_map(
        on_device,
        mesh=mesh,
        in_specs=(
            P("tensor", "dp"),
            P("tensor", "dp"),
            P("dp", "tensor"),
            P("dp", "tensor"),
            P("tensor", "dp"),
        ),
        out_specs=(P("tensor", "dp"), P("dp", "tensor"), P("tensor", "dp")),
        check_vma=False,
    )
```

time: 1210 us -> 93 us (0.08)
  waiting for transfers between devices: 794 us -> 0 us
  blocking collectives: 395 us -> 0 us
  Pallas kernels: 0 us -> 85.5 us
  between operations: 14.8 us -> 0.65 us
    unnamed x3 -> x0, waiting for transfers between devices: 632 us -> none
    all_gather x4 -> x0, blocking collectives: 395 us -> none  [the longest x1 129 us: on_device(): lax.all_gather(activated.astype(jnp.bfloat16), 'dp', axis=0, tiled=True)]
    reduce_scatter x1 -> x0, waiting for transfers between devices: 162 us -> none  [on_device(): lax.psum_scatter(lax.dot_general(block, w_in, (((1,), (1,)), ((), ())), p...]
    pallas_call x0 -> x1, Pallas kernels: none -> 85.5 us  [on_device(): pl.pallas_call(functools.partial(kernel, ny, nz, nx, nh), out_shape=(jax....]
  transfers between devices with their start and end apart: 2 -> 0, of which waited for: 2 -> 0; matrix products, arithmetic and copies ran while one was open for 0% -> 0% of each run, Pallas kernels for 0% -> 0%
where the time goes in v1:
time: 93 us; the launch traced here: 92.7 us
  Pallas kernels  85.5 us (92%)
  local copies, waits for them, and re-layouts  6.52 us (7%)
    pallas_call x1, Pallas kernels, on_device(): pl.pallas_call(functools.partial(kernel, ny, nz, nx, nh), out_shape=(jax....  85.5 us
    unnamed x13, local copies, waits for them, and re-layouts  6.52 us

profile of v1, /device:TPU:1, one launch (start us, length us, event | category | flops | bytes accessed | tf_op | source)
XLA Modules:
  0.0 92.7 jit_solution(16562322657752436205)
XLA Ops:
  0.6 0.0 copy-start
  0.6 1.1 %copy-done = bf16[144,2304]{1,0:T(8,128)(2,1)S(1)} copy-done((bf16[144,2304]{1,0:T(8,128)(2,1)S(1)}, bf16[144,2304]{1,0:T(8,128)(2,1)}, u32[]{:S(2)}) %copy-start) | copy-done | bytes 663576
  1.7 0.0 copy-start.1
  1.7 1.1 %copy-done.1 = bf16[2304,144]{0,1:T(8,128)(2,1)S(1)} copy-done((bf16[2304,144]{0,1:T(8,128)(2,1)S(1)}, bf16[2304,144]{0,1:T(8,128)(2,1)}, u32[]{:S(2)}) %copy-start.1) | copy-done | bytes 663576
  2.8 0.0 copy-start.2
  2.8 0.7 copy-done.2
  3.5 0.0 copy-start.3
  3.5 0.7 copy-done.3
  4.2 0.0 copy-start.4
  4.2 0.7 copy-done.4
  4.9 85.5 %shard_map.76 = (bf16[8,144]{1,0:T(8,128)(2,1)S(1)}, bf16[144,2304]{1,0:T(8,128)(2,1)S(1)}, bf16[144,2304]{1,0:T(8,128)(2,1)S(1)}) custom-call(bf16[8,144]{1,0:T(8,128)(2,1)S(1)} %copy-done.3, bf16[8,144]{1,0:T(8,128)(2,1)S(1)} %copy-done.4, bf16[2,2304]{1,0:T(2,128)(2,1)S(1)} %copy-done.2, bf16[144,2304]{1,0:T(8,128)(2,1)S(1)} %copy-done, ...), custom_call_target="tpu_custom_call" | custom-call | tf_op jit(solution)/shard_map/pallas_call | solution.py:286
  90.4 0.6 copy.11
  91.0 0.8 copy.12
  91.8 0.8 copy.13
Async XLA Ops:
  0.6 1.1 %copy-start = (bf16[144,2304]{1,0:T(8,128)(2,1)S(1)}, bf16[144,2304]{1,0:T(8,128)(2,1)}, u32[]{:S(2)}) copy-start(bf16[144,2304]{1,0:T(8,128)(2,1)} %wi_hbm.1) | copy-start | bytes 1990660
  1.7 1.1 %copy-start.1 = (bf16[2304,144]{0,1:T(8,128)(2,1)S(1)}, bf16[2304,144]{0,1:T(8,128)(2,1)}, u32[]{:S(2)}) copy-start(bf16[2304,144]{0,1:T(8,128)(2,1)} %param.9) | copy-start | bytes 1990660
  2.8 0.7 copy-start.2
  3.5 0.7 copy-start.3
  4.2 0.7 copy-start.4

commit v2 on v1

v2 whole, which is shorter than its diff:
```python
import functools

import jax
import jax.numpy as jnp
from jax import lax
from jax.experimental import pallas as pl
from jax.experimental.pallas import tpu as pltpu
from jax.sharding import PartitionSpec as P

GRID = dict(ny=4, nz=8, nx=4, nh=4)

root_half = 0.7071067811865476
inv_root_two_pi = 0.3989422804014327
bf16, f32 = jnp.bfloat16, jnp.float32


def gelu_parts(saved):
    value = saved.astype(f32)
    cdf = 0.5 * (1.0 + lax.erf(value * root_half))
    density = inv_root_two_pi * jnp.exp(-0.5 * value * value)
    return value * cdf, cdf + value * density


def kernel(
    ny, nz, nx, nh,
    x_hbm, g_hbm, s_hbm, wi_hbm, wo_hbm,
    gin_v, gwi_v, gwo_v,
    rows, own_s, peer_s, wi_v, wo_v, wide, grad_rows, input_rows,
    slope, quad, hid, pre,
    b1_send, b1_recv, b1_own, b2_send, b2_recv, b2_sum, b2_rows, b3_send, b3_own, b3_recv,
    pack, hid_full, pre_full,
    dx_part, dx_send, dx_recv, dz_part, dz_send, dz_recv,
    local_sem, send_sem,
    az_sem, ax_sem, s_sem, hz_sem, hy_sem, hc_sem,
    b1_sem, b2_sem, b3_sem, c1_sem, c2_sem, c3_sem, dx_sem, dz_sem,
):
    dp, tp = lax.axis_index("dp"), lax.axis_index("tensor")
    core = lax.rem(dp, 2)
    chip = lax.div(dp, 2)
    z, y = lax.rem(chip, nz), lax.div(chip, nz)
    x, h = lax.div(tp, nh), lax.rem(tp, nh)
    other = 1 - core

    def at(y=y, z=z, core=core, x=x, h=h):
        return {"dp": (y * nz + z) * 2 + core, "tensor": x * nh + h}

    y_peer = [None] + [at(y=lax.rem(y + k, ny)) for k in range(1, ny)]
    z_peer = [None] + [at(z=lax.rem(z + k, nz)) for k in range(1, nz)]
    x_peer = [None] + [at(x=lax.rem(x + k, nx)) for k in range(1, nx)]
    right, left = at(h=lax.rem(h + 1, nh)), at(h=lax.rem(h + nh - 1, nh))
    partner = at(core=other)
    peers = y_peer[1:] + z_peer[1:] + x_peer[1:] + [right, left, partner]

    half = wi_v.shape[2]

    loads = []

    def load(src, dst):
        copy = pltpu.make_async_copy(src, dst, local_sem.at[len(loads)])
        copy.start()
        loads.append(copy)
        return copy

    load_g = load(g_hbm, rows.at[tp, 0])
    load_x = load(x_hbm, rows.at[tp, 1])
    load_s = [load(s_hbm.at[:, pl.ds(i * half, half)], own_s.at[i]) for i in range(2)]
    load_wo = [load(wo_hbm.at[:, pl.ds(i * half, half)], wo_v.at[i]) for i in range(2)]
    load_wi = [load(wi_hbm.at[:, pl.ds(i * half, half)], wi_v.at[i]) for i in range(2)]

    barrier = pltpu.get_barrier_semaphore()
    for peer in peers:
        pl.semaphore_signal(barrier, inc=1, device_id=peer, device_id_type=pl.DeviceIdType.MESH)
    pl.semaphore_wait(barrier, len(peers))

    sends = []
    pending = {}

    def send(src, dst, recv_sem, peer):
        pending[(id(recv_sem[0]), recv_sem[1:])] = (dst, recv_sem)
        recv_sem = recv_sem[0].at[recv_sem[1:]]
        copy = pltpu.make_async_remote_copy(
            src_ref=src, dst_ref=dst, send_sem=send_sem.at[len(sends)], recv_sem=recv_sem,
            device_id=peer, device_id_type=pl.DeviceIdType.MESH,
        )
        copy.start()
        sends.append(copy)

    def arrived(dst, recv_sem):
        pending.pop((id(recv_sem[0]), recv_sem[1:]))
        recv_sem = recv_sem[0].at[recv_sem[1:]]
        pltpu.make_async_remote_copy(
            src_ref=dst, dst_ref=dst, send_sem=send_sem.at[0], recv_sem=recv_sem,
            device_id=partner, device_id_type=pl.DeviceIdType.MESH,
        ).wait_recv()

    slot = lambda x_, h_: x_ * nh + h_
    h_left, h_right, h_far = lax.rem(h + nh - 1, nh), lax.rem(h + 1, nh), lax.rem(h + 2, nh)

    def to_x(which, h_):
        block = rows.at[slot(x, h_)]
        for k in range(1, nx):
            send(block, block, (ax_sem, k - 1, which), x_peer[k])

    load_g.wait()
    load_x.wait()
    mine = rows.at[tp]
    send(mine, mine, (az_sem, 0), right)
    send(mine, mine, (az_sem, 1), left)

    for copy in load_s:
        copy.wait()
    send(own_s.at[other], peer_s, (s_sem, 0), partner)
    to_x(0, h)

    arrived(peer_s, (s_sem, 0))
    own, peer = gelu_parts(own_s[core]), gelu_parts(peer_s[...])
    n = own[0].shape[0]
    first = core == 0
    for ref, i in ((quad, 0), (slope, 1)):
        ref[0:n, :] = jnp.where(first, own[i], peer[i])
        ref[n : 2 * n, :] = jnp.where(first, peer[i], own[i])
    hid[core, y, z] = quad[...].astype(bf16)

    def to_z(buf, sem):
        block = buf.at[core, y, z]
        for k in range(1, nz):
            send(block, block, (sem, k - 1), z_peer[k])

    def from_z(buf, sem):
        for k in range(1, nz):
            arrived(buf.at[core, y, lax.rem(z + nz - k, nz)], (sem, k - 1))

    def to_y(buf, sem):
        block = buf.at[core, y]
        for k in range(1, ny):
            send(block, block, (sem, k - 1), y_peer[k])

    def from_y(buf, sem, k):
        arrived(buf.at[core, lax.rem(y + ny - k, ny)], (sem, k - 1))

    from_left = rows.at[slot(x, h_left)]
    arrived(from_left, (az_sem, 0))
    send(from_left, from_left, (az_sem, 2), right)
    to_x(1, h_left)
    arrived(rows.at[slot(x, h_right)], (az_sem, 1))
    to_x(2, h_right)
    near, step = nh - 1, rows.shape[2]
    groups = (h, h_left, h_right, h_far)

    def from_x(which):
        for k in range(1, nx):
            arrived(rows.at[slot(lax.rem(x + nx - k, nx), groups[which])], (ax_sem, k - 1, which))

    def product(lo, hi):
        count = (hi - lo) * nx
        for g in range(lo, hi):
            for x_ in range(nx):
                r = ((g - lo) * nx + x_) * step
                wide[r : r + step, :] = rows[slot(x_, groups[g]), 0].astype(f32)
        lhs = wide[0 : count * step, :].astype(bf16)

        def place(ref, which):
            out = jnp.dot(lhs, wo_v[which], preferred_element_type=f32).reshape(count, step, half)
            for g in range(lo, hi):
                for x_ in range(nx):
                    ref[x_, g] = out[(g - lo) * nx + x_].astype(ref.dtype)

        place(b1_send, other)
        for k in order:
            y_ = lax.rem(y + k, ny)
            send(b1_send.at[y_, lo:hi], b1_recv.at[y_, lo:hi], (b1_sem, k, lo), partner)
        place(b1_own, core)

    def fold(lo, hi):
        for k in order:
            y_ = lax.rem(y + k, ny)
            arrived(b1_recv.at[y_, lo:hi], (b1_sem, k, lo))
            total = b1_own[y_, lo:hi] + b1_recv[y_, lo:hi].astype(f32)
            if k:
                b2_send[k - 1, lo:hi] = total.astype(bf16)
                send(b2_send.at[k - 1, lo:hi], b2_recv.at[k - 1, lo:hi], (b2_sem, k - 1, lo), y_peer[k])
            else:
                b2_sum[lo:hi] = total

    order = list(range(1, ny)) + [0]
    for which in range(near):
        from_x(which)
    for copy in load_wo:
        copy.wait()
    product(0, near)
    fold(0, near)
    arrived(rows.at[slot(x, h_far)], (az_sem, 2))
    to_x(near, h_far)
    from_x(near)
    product(near, nh)
    fold(near, nh)
    to_z(hid, hz_sem)
    for lo, hi in ((0, near), (near, nh)):
        for k in range(1, ny):
            arrived(b2_recv.at[k - 1, lo:hi], (b2_sem, k - 1, lo))
        for g in range(lo, hi):
            total = b2_sum[g]
            for k in range(1, ny):
                total = total + b2_recv[k - 1, g].astype(f32)
            b2_rows[pl.ds(pl.multiple_of(groups[g] * step, step), step), :] = total
    deep = b3_own.shape[1]
    for j in range(nz):
        piece = b2_rows[j * deep : (j + 1) * deep, :]
        b3_own[j] = piece
        b3_send[j] = piece.astype(bf16)
    for k in range(1, nz):
        send(b3_send.at[lax.rem(z + k, nz)], b3_recv.at[k - 1], (b3_sem, k - 1), z_peer[k])
    from_z(hid, hz_sem)
    to_y(hid, hy_sem)
    total = b3_own[z]
    for k in range(1, nz):
        arrived(b3_recv.at[k - 1], (b3_sem, k - 1))
        total = total + b3_recv[k - 1].astype(f32)
    pre[core, y, z] = (total * slope[...]).astype(bf16)
    def gathered(which, out):
        for t in range(rows.shape[0]):
            wide[t * step : (t + 1) * step, :] = rows[t, which].astype(f32)
        out[...] = wide[...].astype(bf16)

    to_z(pre, c1_sem)
    gathered(0, grad_rows)
    gathered(1, input_rows)
    from_z(pre, c1_sem)
    to_y(pre, c2_sem)
    send(pre.at[core, y], pre.at[core, y], (c3_sem, 0), partner)
    for k in range(1, ny):
        from_y(pre, c2_sem, k)
        block = pre.at[core, lax.rem(y + ny - k, ny)]
        send(block, block, (c3_sem, k), partner)

    for k in range(1, ny):
        from_y(hid, hy_sem, k)
    send(hid.at[core], hid.at[core], (hc_sem, 0), partner)

    def packed(buf, which, out):
        for i in range(ny):
            for j in range(nz):
                r = (i * nz + j) * deep
                pack[r : r + deep, :] = buf[which, i, j].astype(f32)
        out[which] = pack[...].astype(bf16)

    def back(which):
        return lax.dot_general(
            pre_full[which], wi_v[which], (((1,), (1,)), ((), ())), preferred_element_type=f32
        )

    for copy in load_wi:
        copy.wait()
    packed(pre, core, pre_full)
    part = back(core)
    for k in range(ny):
        arrived(pre.at[other, lax.rem(y + ny - k, ny)], (c3_sem, k))
    packed(pre, other, pre_full)
    part = part + back(other)
    dx_part[...] = part.reshape(dx_part.shape)
    for k in range(1, nx):
        dx_send[k - 1] = dx_part[lax.rem(x + k, nx)].astype(bf16)
        send(dx_send.at[k - 1], dx_recv.at[k - 1], (dx_sem, k - 1), x_peer[k])
    arrived(hid.at[other], (hc_sem, 0))
    packed(hid, 0, hid_full)
    packed(hid, 1, hid_full)
    total = dx_part[x]
    for k in range(1, nx):
        arrived(dx_recv.at[k - 1], (dx_sem, k - 1))
        total = total + dx_recv[k - 1].astype(f32)
    dz_part[...] = total.reshape(dz_part.shape)
    dz_send[0] = dz_part[h_far].astype(bf16)
    dz_send[1] = dz_part[h_left].astype(bf16)
    send(dz_send.at[0], dz_recv.at[0], (dz_sem, 0), right)
    send(dz_send.at[1], dz_recv.at[1], (dz_sem, 1), left)

    def outer(a, b):
        return lax.dot_general(
            a[...], b, (((0,), (0,)), ((), ())), preferred_element_type=f32
        ).astype(bf16)

    for i in range(2):
        gwi_v[:, i * half : (i + 1) * half] = outer(input_rows, pre_full[i])
    arrived(dz_recv.at[0], (dz_sem, 0))
    dz_send[2] = (dz_part[h_right] + dz_recv[0].astype(f32)).astype(bf16)
    send(dz_send.at[2], dz_recv.at[2], (dz_sem, 2), right)
    for i in range(2):
        gwo_v[:, i * half : (i + 1) * half] = outer(grad_rows, hid_full[i])
    arrived(dz_recv.at[1], (dz_sem, 1))
    arrived(dz_recv.at[2], (dz_sem, 2))
    gin_v[...] = (dz_part[h] + dz_recv[1].astype(f32) + dz_recv[2].astype(f32)).astype(bf16)
    for copy in sends:
        copy.wait_send()


def put(*refs):
    sems = refs[6]
    copies = [pltpu.make_async_copy(refs[i], refs[3 + i], sems.at[i]) for i in range(3)]
    for copy in copies:
        copy.start()
    for copy in copies:
        copy.wait()


def on_device(inputs, grad_out, saved_pre, w_in, w_out):
    ny, nz, nx, nh = (GRID[k] for k in ("ny", "nz", "nx", "nh"))
    step, width = inputs.shape
    n, hidden = saved_pre.shape
    half = hidden // 2
    tokens = step * nx * nh
    deep = tokens // (ny * nz)
    per_y, per_x = tokens // ny, tokens // nx
    vmem, dma = pltpu.VMEM, pltpu.SemaphoreType.DMA
    shapes = ((step, width), (width, hidden), (width, hidden))
    any_space = pl.BlockSpec(memory_space=pl.ANY)
    n_sends = ny + ny - 1 + 3 + 4 * (nx - 1) + 1 + 3 * (nz - 1) + 3 * (ny - 1) + ny + 1 + ny + (nx - 1) + 3
    results = pl.pallas_call(
        functools.partial(kernel, ny, nz, nx, nh),
        out_shape=tuple(vmem(shape, bf16) for shape in shapes),
        in_specs=[any_space] * 5,
        out_specs=(pl.BlockSpec(memory_space=vmem),) * 3,
        scratch_shapes=[
            vmem((nx * nh, 2, step, width), bf16),
            vmem((2, n, half), bf16),
            vmem((n, half), bf16),
            vmem((2, width, half), bf16),
            vmem((2, width, half), bf16),
            vmem((tokens, width), f32),
            vmem((tokens, width), bf16),
            vmem((tokens, width), bf16),
            vmem((deep, half), f32),
            vmem((deep, half), f32),
            vmem((2, ny, nz, deep, half), bf16),
            vmem((2, ny, nz, deep, half), bf16),
            vmem((ny, nh, step, half), bf16),
            vmem((ny, nh, step, half), bf16),
            vmem((ny, nh, step, half), f32),
            vmem((ny - 1, nh, step, half), bf16),
            vmem((ny - 1, nh, step, half), bf16),
            vmem((nh, step, half), f32),
            vmem((per_y, half), f32),
            vmem((nz, deep, half), bf16),
            vmem((nz, deep, half), f32),
            vmem((nz - 1, deep, half), bf16),
            vmem((tokens, half), f32),
            vmem((2, tokens, half), bf16),
            vmem((2, tokens, half), bf16),
            vmem((nx, per_x, width), f32),
            vmem((nx - 1, per_x, width), bf16),
            vmem((nx - 1, per_x, width), bf16),
            vmem((nh, step, width), f32),
            vmem((3, step, width), bf16),
            vmem((3, step, width), bf16),
            dma((11,)),
            dma((n_sends,)),
            dma((3,)),
            dma((nx - 1, 4)),
            dma((1,)),
            dma((nz - 1,)),
            dma((ny - 1,)),
            dma((1,)),
            dma((ny, nh)),
            dma((ny - 1, nh)),
            dma((nz - 1,)),
            dma((nz - 1,)),
            dma((ny - 1,)),
            dma((ny,)),
            dma((nx - 1,)),
            dma((3,)),
        ],
        compiler_params=pltpu.CompilerParams(
            collective_id=0, has_side_effects=True
        ),
    )(inputs, grad_out, saved_pre, w_in, w_out.T)
    grad_in, grad_w_in, grad_w_out = pl.pallas_call(
        put,
        out_shape=tuple(jax.ShapeDtypeStruct(shape, bf16) for shape in shapes),
        in_specs=[pl.BlockSpec(memory_space=vmem)] * 3,
        out_specs=(any_space,) * 3,
        scratch_shapes=[dma((3,))],
    )(*[pltpu.with_memory_space_constraint(r, vmem) for r in results])
    return grad_in, grad_w_in, grad_w_out.T


def solution(mesh):
    return jax.shard_map(
        on_device,
        mesh=mesh,
        in_specs=(
            P("tensor", "dp"),
            P("tensor", "dp"),
            P("dp", "tensor"),
            P("dp", "tensor"),
            P("tensor", "dp"),
        ),
        out_specs=(P("tensor", "dp"), P("dp", "tensor"), P("tensor", "dp")),
        check_vma=False,
    )
```

time: 93 us -> 85.5 us (0.919)
  local copies, waits for them, and re-layouts: 6.52 us -> 0 us
    unnamed x13 -> x0, local copies, waits for them, and re-layouts: 6.52 us -> none
    pallas_call x1 -> x2, Pallas kernels: 85.5 us -> 84.8 us  [the longest x1 83.7 us: on_device(): pl.pallas_call(functools.partial(kernel, ny, nz, nx, nh), out_shape=tuple...]
where the time goes in v2:
time: 85.5 us; the launch traced here: 85.4 us
  Pallas kernels  84.8 us (99%)
    pallas_call x1, Pallas kernels, on_device(): pl.pallas_call(functools.partial(kernel, ny, nz, nx, nh), out_shape=tuple...  83.7 us

profile of v2, /device:TPU:1, one launch (start us, length us, event | category | flops | bytes accessed | tf_op | source)
XLA Modules:
  0.0 85.4 jit_solution(3320537953832071241)
XLA Ops:
  0.6 83.7 %shard_map.76 = (bf16[8,144]{1,0:T(8,128)(2,1)S(1)}, bf16[144,2304]{1,0:T(8,128)(2,1)S(1)}, bf16[144,2304]{1,0:T(8,128)(2,1)S(1)}) custom-call(bf16[8,144]{1,0:T(8,128)(2,1)} %x_hbm.1, bf16[8,144]{1,0:T(8,128)(2,1)} %g_hbm.1, bf16[2,2304]{1,0:T(2,128)(2,1)} %s_hbm.1, bf16[144,2304]{1,0:T(8,128)(2,1)} %wi_hbm.1, bf16[144,2304]{1,0:T(8,128)(2,1)} %bitcast.2), custom_call_target="tpu_custom_call" | custom-call | tf_op jit(solution)/shard_map/pallas_call | solution.py:317
  84.3 1.1 %shard_map.77 = (bf16[8,144]{1,0:T(8,128)(2,1)}, bf16[144,2304]{1,0:T(8,128)(2,1)}, bf16[144,2304]{1,0:T(8,128)(2,1)}) custom-call(bf16[8,144]{1,0:T(8,128)(2,1)S(1)} %get-tuple-element.9.refs_0_, bf16[144,2304]{1,0:T(8,128)(2,1)S(1)} %get-tuple-element.10.refs_1_, bf16[144,2304]{1,0:T(8,128)(2,1)S(1)} %get-tuple-element.11.refs_2_), custom_call_target="tpu_custom_call" | custom-call | tf_op jit(solution)/shard_map/pallas_call | solution.py:375

commit v3 on v2

v3 whole, which is shorter than its diff:
```python
import functools

import jax
import jax.numpy as jnp
from jax import lax
from jax.experimental import pallas as pl
from jax.experimental.pallas import tpu as pltpu
from jax.sharding import PartitionSpec as P

GRID = dict(ny=4, nz=8, nx=4, nh=4)

root_half = 0.7071067811865476
inv_root_two_pi = 0.3989422804014327
bf16, f32 = jnp.bfloat16, jnp.float32


def gelu_parts(saved):
    value = saved.astype(f32)
    cdf = 0.5 * (1.0 + lax.erf(value * root_half))
    density = inv_root_two_pi * jnp.exp(-0.5 * value * value)
    return value * cdf, cdf + value * density


def kernel(
    ny, nz, nx, nh,
    x_hbm, g_hbm, s_hbm, wi_hbm, wo_hbm,
    gin_v, gwi_v, gwo_v,
    rows, own_s, peer_s, wi_v, wo_v, wide, grad_rows, input_rows,
    slope, quad, hid, pre,
    b1_send, b1_recv, b1_own, b2_send, b2_recv, b2_sum, b2_rows, b3_send, b3_own, b3_recv,
    pack, hid_full, pre_full,
    fx_part, fx_send, fx_recv, dx_part, dx_send, dx_recv, dz_part, dz_send, dz_recv,
    local_sem, send_sem,
    az_sem, ax_sem, s_sem, hz_sem, hy_sem, hc_sem,
    b1_sem, b2_sem, b3_sem, c1_sem, c2_sem, c3_sem, dx_sem, dz_sem,
):
    dp, tp = lax.axis_index("dp"), lax.axis_index("tensor")
    core = lax.rem(dp, 2)
    chip = lax.div(dp, 2)
    z, y = lax.rem(chip, nz), lax.div(chip, nz)
    x, h = lax.div(tp, nh), lax.rem(tp, nh)
    other = 1 - core

    def at(y=y, z=z, core=core, x=x, h=h):
        return {"dp": (y * nz + z) * 2 + core, "tensor": x * nh + h}

    y_peer = [None] + [at(y=lax.rem(y + k, ny)) for k in range(1, ny)]
    z_peer = [None] + [at(z=lax.rem(z + k, nz)) for k in range(1, nz)]
    x_peer = [None] + [at(x=lax.rem(x + k, nx)) for k in range(1, nx)]
    right, left = at(h=lax.rem(h + 1, nh)), at(h=lax.rem(h + nh - 1, nh))
    partner = at(core=other)
    peers = y_peer[1:] + z_peer[1:] + x_peer[1:] + [right, left, partner]

    half = wi_v.shape[2]

    def load(src, dst, i):
        copy = pltpu.make_async_copy(src, dst, local_sem.at[i])
        copy.start()
        return copy

    load_g = load(g_hbm, rows.at[tp, 0], 0)
    load_x = load(x_hbm, rows.at[tp, 1], 1)
    for i in range(2):
        columns = pl.ds(i * half, half)
        for hbm, ref, sem in ((s_hbm, own_s, 2), (wo_hbm, wo_v, 3), (wi_hbm, wi_v, 4)):
            load(hbm.at[:, columns], ref.at[i], sem)

    def loaded(ref, sem):
        pltpu.make_async_copy(ref, ref, local_sem.at[sem]).wait()

    barrier = pltpu.get_barrier_semaphore()
    for peer in peers:
        pl.semaphore_signal(barrier, inc=1, device_id=peer, device_id_type=pl.DeviceIdType.MESH)
    pl.semaphore_wait(barrier, len(peers))

    def send(src, dst, group, recv_sem, peer):
        pltpu.make_async_remote_copy(
            src_ref=src, dst_ref=dst, send_sem=send_sem.at[group], recv_sem=recv_sem,
            device_id=peer, device_id_type=pl.DeviceIdType.MESH,
        ).start()

    def handle(ref, group, recv_sem):
        return pltpu.make_async_remote_copy(
            src_ref=ref, dst_ref=ref, send_sem=send_sem.at[group], recv_sem=recv_sem,
            device_id=partner, device_id_type=pl.DeviceIdType.MESH,
        )

    def arrived(ref, recv_sem):
        handle(ref, 0, recv_sem).wait_recv()

    slot = lambda x_, h_: x_ * nh + h_
    h_left, h_right, h_far = lax.rem(h + nh - 1, nh), lax.rem(h + 1, nh), lax.rem(h + 2, nh)

    def to_x(which, h_):
        block = rows.at[slot(x, h_)]
        for k in range(1, nx):
            send(block, block, 0, ax_sem.at[0 if which < nh - 1 else 1], x_peer[k])

    load_g.wait()
    load_x.wait()
    mine = rows.at[tp]
    send(mine, mine, 0, az_sem.at[0], right)
    send(mine, mine, 0, az_sem.at[1], left)

    loaded(own_s, 2)
    send(own_s.at[other], peer_s, 1, s_sem.at[0], partner)
    to_x(0, h)

    arrived(peer_s, s_sem.at[0])
    own, peer = gelu_parts(own_s[core]), gelu_parts(peer_s[...])
    n = own[0].shape[0]
    first = core == 0
    for ref, i in ((quad, 0), (slope, 1)):
        ref[0:n, :] = jnp.where(first, own[i], peer[i])
        ref[n : 2 * n, :] = jnp.where(first, peer[i], own[i])
    hid[core, y, z] = quad[...].astype(bf16)

    def to_z(buf, group, sem):
        block = buf.at[core, y, z]
        for k in range(1, nz):
            send(block, block, group, sem.at[0], z_peer[k])

    def from_z(buf, sem):
        arrived(buf.at[core, y, 0 : nz - 1], sem.at[0])

    from_left = rows.at[slot(x, h_left)]
    arrived(from_left, az_sem.at[0])
    send(from_left, from_left, 0, az_sem.at[2], right)
    to_x(1, h_left)
    arrived(rows.at[slot(x, h_right)], az_sem.at[1])
    to_x(2, h_right)
    near, step = nh - 1, rows.shape[2]
    groups = (h, h_left, h_right, h_far)

    def product(lo, hi):
        count = (hi - lo) * nx
        for g in range(lo, hi):
            for x_ in range(nx):
                r = ((g - lo) * nx + x_) * step
                wide[r : r + step, :] = rows[slot(x_, groups[g]), 0].astype(f32)
        lhs = wide[0 : count * step, :].astype(bf16)

        def place(ref, which):
            out = jnp.dot(lhs, wo_v[which], preferred_element_type=f32).reshape(count, step, half)
            for g in range(lo, hi):
                for x_ in range(nx):
                    ref[x_, g] = out[(g - lo) * nx + x_].astype(ref.dtype)

        place(b1_send, other)
        for k in order:
            y_ = lax.rem(y + k, ny)
            send(b1_send.at[y_, lo:hi], b1_recv.at[y_, lo:hi], 2, b1_sem.at[ny if lo else k], partner)
        place(b1_own, core)

    def fold(lo, hi):
        if lo:
            arrived(b1_recv.at[:, lo:hi], b1_sem.at[ny])
        for k in order:
            y_ = lax.rem(y + k, ny)
            if lo == 0:
                arrived(b1_recv.at[y_, lo:hi], b1_sem.at[k])
            total = b1_own[y_, lo:hi] + b1_recv[y_, lo:hi].astype(f32)
            if k:
                b2_send[k - 1, lo:hi] = total.astype(bf16)
                send(b2_send.at[k - 1, lo:hi], b2_recv.at[k - 1, lo:hi], 3, b2_sem.at[1 if lo else 0], y_peer[k])
            else:
                b2_sum[lo:hi] = total

    order = list(range(1, ny)) + [0]
    arrived(rows.at[0 : near * (nx - 1)], ax_sem.at[0])
    loaded(wo_v, 3)
    product(0, near)
    fold(0, near)
    arrived(rows.at[slot(x, h_far)], az_sem.at[2])
    to_x(near, h_far)
    arrived(rows.at[0 : nx - 1], ax_sem.at[1])
    product(near, nh)
    fold(near, nh)
    to_z(hid, 5, hz_sem)
    for lo, hi in ((0, near), (near, nh)):
        arrived(b2_recv.at[:, lo:hi], b2_sem.at[1 if lo else 0])
        for g in range(lo, hi):
            total = b2_sum[g]
            for k in range(1, ny):
                total = total + b2_recv[k - 1, g].astype(f32)
            b2_rows[pl.ds(pl.multiple_of(groups[g] * step, step), step), :] = total
    deep = b3_own.shape[1]
    for j in range(nz):
        piece = b2_rows[j * deep : (j + 1) * deep, :]
        b3_own[j] = piece
        b3_send[j] = piece.astype(bf16)
    for k in range(1, nz):
        send(b3_send.at[lax.rem(z + k, nz)], b3_recv.at[k - 1], 4, b3_sem.at[0], z_peer[k])
    from_z(hid, hz_sem)
    for k in range(1, ny):
        send(hid.at[core, y], hid.at[core, y], 7, hy_sem.at[0], y_peer[k])
    total = b3_own[z]
    arrived(b3_recv, b3_sem.at[0])
    for k in range(1, nz):
        total = total + b3_recv[k - 1].astype(f32)
    pre[core, y, z] = (total * slope[...]).astype(bf16)
    def gathered(which, out):
        for t in range(rows.shape[0]):
            wide[t * step : (t + 1) * step, :] = rows[t, which].astype(f32)
        out[...] = wide[...].astype(bf16)

    to_z(pre, 6, c1_sem)
    gathered(0, grad_rows)
    gathered(1, input_rows)
    from_z(pre, c1_sem)
    per = step // deep
    far_first = (near,) + tuple(range(near))

    def part_of(half_, y_, g):
        return pre.at[half_, y_, pl.ds(groups[g] * per, per)]

    def y_back(k):
        return lax.rem(y + ny - k, ny)

    for g in far_first:
        block = part_of(core, y, g)
        for k in range(1, ny):
            send(block, block, 9, c2_sem.at[k - 1 if g == near else ny - 1], y_peer[k])
        send(block, block, 10, c3_sem.at[0 if g == near else 1], partner)

    def packed(buf, which, out):
        for i in range(ny):
            for j in range(nz):
                r = (i * nz + j) * deep
                pack[r : r + deep, :] = buf[which, i, j].astype(f32)
        out[which] = pack[...].astype(bf16)

    def back(lhs, which):
        return lax.dot_general(lhs, wi_v[which], (((1,), (1,)), ((), ())), preferred_element_type=f32)

    def far_back(which):
        for i in range(ny):
            for j in range(per):
                r = i * step + j * deep
                pack[r : r + deep, :] = pre[which, i, h_far * per + j].astype(f32)
        return back(pack[0 : ny * step, :].astype(bf16), which)

    for k in range(1, ny):
        block = part_of(core, y_back(k), near)
        arrived(block, c2_sem.at[k - 1])
        send(block, block, 10, c3_sem.at[0], partner)
    loaded(wi_v, 4)
    part = far_back(core)
    arrived(pre.at[other, :, 0:per], c3_sem.at[0])
    part = part + far_back(other)

    fx_part[...] = part.reshape(fx_part.shape)
    for k in range(1, nx):
        fx_send[k - 1] = fx_part[lax.rem(x + k, nx)].astype(bf16)
        send(fx_send.at[k - 1], fx_recv.at[k - 1], 11, dx_sem.at[1], x_peer[k])
    arrived(pre.at[core, 0 : ny - 1, 0 : near * per], c2_sem.at[ny - 1])
    for g in range(near):
        for k in range(1, ny):
            block = part_of(core, y_back(k), g)
            send(block, block, 10, c3_sem.at[1], partner)
    arrived(hid.at[core, 0 : ny - 1], hy_sem.at[0])
    send(hid.at[core], hid.at[core], 8, hc_sem.at[0], partner)
    total = fx_part[x]
    arrived(fx_recv, dx_sem.at[1])
    for k in range(1, nx):
        total = total + fx_recv[k - 1].astype(f32)
    dz_send[0] = total.astype(bf16)
    send(dz_send.at[0], dz_recv.at[0], 13, dz_sem.at[0], right)
    packed(pre, core, pre_full)
    part = back(pre_full[core], core)
    arrived(pre.at[other, :, 0 : near * per], c3_sem.at[1])
    packed(pre, other, pre_full)
    part = part + back(pre_full[other], other)
    dx_part[...] = part.reshape(dx_part.shape)
    for k in range(1, nx):
        for g in range(near):
            dx_send[k - 1, g] = dx_part[lax.rem(x + k, nx), groups[g]].astype(bf16)
        send(dx_send.at[k - 1], dx_recv.at[k - 1], 12, dx_sem.at[0], x_peer[k])
    arrived(dx_recv, dx_sem.at[0])
    for g in range(near):
        total = dx_part[x, groups[g]]
        for k in range(1, nx):
            total = total + dx_recv[k - 1, g].astype(f32)
        dz_part[g] = total
    dz_send[1] = dz_part[1].astype(bf16)
    send(dz_send.at[1], dz_recv.at[1], 13, dz_sem.at[1], left)
    arrived(dz_recv.at[0], dz_sem.at[0])
    dz_send[2] = (dz_part[2] + dz_recv[0].astype(f32)).astype(bf16)
    send(dz_send.at[2], dz_recv.at[2], 13, dz_sem.at[2], right)

    def outer(a, b):
        return lax.dot_general(
            a[...], b, (((0,), (0,)), ((), ())), preferred_element_type=f32
        ).astype(bf16)

    for i in range(2):
        gwi_v[:, i * half : (i + 1) * half] = outer(input_rows, pre_full[i])
    arrived(hid.at[other], hc_sem.at[0])
    for i in range(2):
        packed(hid, i, hid_full)
        gwo_v[:, i * half : (i + 1) * half] = outer(grad_rows, hid_full[i])
    arrived(dz_recv.at[1], dz_sem.at[1])
    arrived(dz_recv.at[2], dz_sem.at[2])
    gin_v[...] = (dz_part[0] + dz_recv[1].astype(f32) + dz_recv[2].astype(f32)).astype(bf16)
    sent = (
        rows.at[0 : 3 + nh * (nx - 1)], peer_s, b1_send, b2_send, b3_send.at[0 : nz - 1],
        hid.at[core, y, 0 : nz - 1], pre.at[core, y, 0 : nz - 1], hid.at[core, 0 : ny - 1],
        hid.at[core], pre.at[core, 0 : ny - 1], pre.at[core], fx_send, dx_send, dz_send,
    )
    for group, ref in enumerate(sent):
        handle(ref, group, s_sem.at[0]).wait_send()


def put(*refs):
    sems = refs[6]
    copies = [pltpu.make_async_copy(refs[i], refs[3 + i], sems.at[i]) for i in range(3)]
    for copy in copies:
        copy.start()
    for copy in copies:
        copy.wait()


def on_device(inputs, grad_out, saved_pre, w_in, w_out):
    ny, nz, nx, nh = (GRID[k] for k in ("ny", "nz", "nx", "nh"))
    step, width = inputs.shape
    n, hidden = saved_pre.shape
    half = hidden // 2
    tokens = step * nx * nh
    deep = tokens // (ny * nz)
    per_y = tokens // ny
    vmem, dma = pltpu.VMEM, pltpu.SemaphoreType.DMA
    shapes = ((step, width), (width, hidden), (width, hidden))
    any_space = pl.BlockSpec(memory_space=pl.ANY)
    results = pl.pallas_call(
        functools.partial(kernel, ny, nz, nx, nh),
        out_shape=tuple(vmem(shape, bf16) for shape in shapes),
        in_specs=[any_space] * 5,
        out_specs=(pl.BlockSpec(memory_space=vmem),) * 3,
        scratch_shapes=[
            vmem((nx * nh, 2, step, width), bf16),
            vmem((2, n, half), bf16),
            vmem((n, half), bf16),
            vmem((2, width, half), bf16),
            vmem((2, width, half), bf16),
            vmem((tokens, width), f32),
            vmem((tokens, width), bf16),
            vmem((tokens, width), bf16),
            vmem((deep, half), f32),
            vmem((deep, half), f32),
            vmem((2, ny, nz, deep, half), bf16),
            vmem((2, ny, nz, deep, half), bf16),
            vmem((ny, nh, step, half), bf16),
            vmem((ny, nh, step, half), bf16),
            vmem((ny, nh, step, half), f32),
            vmem((ny - 1, nh, step, half), bf16),
            vmem((ny - 1, nh, step, half), bf16),
            vmem((nh, step, half), f32),
            vmem((per_y, half), f32),
            vmem((nz, deep, half), bf16),
            vmem((nz, deep, half), f32),
            vmem((nz - 1, deep, half), bf16),
            vmem((tokens, half), f32),
            vmem((2, tokens, half), bf16),
            vmem((2, tokens, half), bf16),
            vmem((nx, step, width), f32),
            vmem((nx - 1, step, width), bf16),
            vmem((nx - 1, step, width), bf16),
            vmem((nx, nh, step, width), f32),
            vmem((nx - 1, nh - 1, step, width), bf16),
            vmem((nx - 1, nh - 1, step, width), bf16),
            vmem((nh - 1, step, width), f32),
            vmem((3, step, width), bf16),
            vmem((3, step, width), bf16),
            dma((5,)),
            dma((14,)),
            dma((3,)),
            dma((2,)),
            dma((1,)),
            dma((1,)),
            dma((1,)),
            dma((1,)),
            dma((ny + 1,)),
            dma((2,)),
            dma((1,)),
            dma((1,)),
            dma((ny,)),
            dma((2,)),
            dma((2,)),
            dma((3,)),
        ],
        compiler_params=pltpu.CompilerParams(
            collective_id=0, has_side_effects=True
        ),
    )(inputs, grad_out, saved_pre, w_in, w_out.T)
    grad_in, grad_w_in, grad_w_out = pl.pallas_call(
        put,
        out_shape=tuple(jax.ShapeDtypeStruct(shape, bf16) for shape in shapes),
        in_specs=[pl.BlockSpec(memory_space=vmem)] * 3,
        out_specs=(any_space,) * 3,
        scratch_shapes=[dma((3,))],
    )(*[pltpu.with_memory_space_constraint(r, vmem) for r in results])
    return grad_in, grad_w_in, grad_w_out.T


def solution(mesh):
    return jax.shard_map(
        on_device,
        mesh=mesh,
        in_specs=(
            P("tensor", "dp"),
            P("tensor", "dp"),
            P("dp", "tensor"),
            P("dp", "tensor"),
            P("tensor", "dp"),
        ),
        out_specs=(P("tensor", "dp"), P("dp", "tensor"), P("tensor", "dp")),
        check_vma=False,
    )
```

time: 85.5 us -> 82.7 us (0.967)
  Pallas kernels: 84.8 us -> 82 us
    pallas_call x1, Pallas kernels: 83.7 us -> 80.9 us  [on_device(): pl.pallas_call(functools.partial(kernel, ny, nz, nx, nh), out_shape=tuple...]
where the time goes in v3:
time: 82.7 us; the launch traced here: 82.6 us
  Pallas kernels  82 us (99%)
    pallas_call x1, Pallas kernels, on_device(): pl.pallas_call(functools.partial(kernel, ny, nz, nx, nh), out_shape=tuple...  80.9 us

profile of v3, /device:TPU:1, one launch (start us, length us, event | category | flops | bytes accessed | tf_op | source)
XLA Modules:
  0.0 82.6 jit_solution(5319933851143073460)
XLA Ops:
  0.6 80.9 %shard_map.76 = (bf16[8,144]{1,0:T(8,128)(2,1)S(1)}, bf16[144,2304]{1,0:T(8,128)(2,1)S(1)}, bf16[144,2304]{1,0:T(8,128)(2,1)S(1)}) custom-call(bf16[8,144]{1,0:T(8,128)(2,1)} %x_hbm.1, bf16[8,144]{1,0:T(8,128)(2,1)} %g_hbm.1, bf16[2,2304]{1,0:T(2,128)(2,1)} %s_hbm.1, bf16[144,2304]{1,0:T(8,128)(2,1)} %wi_hbm.1, bf16[144,2304]{1,0:T(8,128)(2,1)} %bitcast.2), custom_call_target="tpu_custom_call" | custom-call | tf_op jit(solution)/shard_map/pallas_call | solution.py:334
  81.5 1.1 %shard_map.77 = (bf16[8,144]{1,0:T(8,128)(2,1)}, bf16[144,2304]{1,0:T(8,128)(2,1)}, bf16[144,2304]{1,0:T(8,128)(2,1)}) custom-call(bf16[8,144]{1,0:T(8,128)(2,1)S(1)} %get-tuple-element.9.refs_0_, bf16[144,2304]{1,0:T(8,128)(2,1)S(1)} %get-tuple-element.10.refs_1_, bf16[144,2304]{1,0:T(8,128)(2,1)S(1)} %get-tuple-element.11.refs_2_), custom_call_target="tpu_custom_call" | custom-call | tf_op jit(solution)/shard_map/pallas_call | solution.py:395

commit v4 on v3

--- a/solution.py
+++ b/solution.py
@@ -26,12 +26,12 @@
     x_hbm, g_hbm, s_hbm, wi_hbm, wo_hbm,
     gin_v, gwi_v, gwo_v,
     rows, own_s, peer_s, wi_v, wo_v, wide, grad_rows, input_rows,
-    slope, quad, hid, pre,
-    b1_send, b1_recv, b1_own, b2_send, b2_recv, b2_sum, b2_rows, b3_send, b3_own, b3_recv,
+    slope, quad, saved_send, saved_recv, hid, pre,
+    b1_send, b1_recv, b1_own, b2_send, b2_recv, b2_sum, b3_send, b3_own, b3_recv,
     pack, hid_full, pre_full,
     fx_part, fx_send, fx_recv, dx_part, dx_send, dx_recv, dz_part, dz_send, dz_recv,
     local_sem, send_sem,
-    az_sem, ax_sem, s_sem, hz_sem, hy_sem, hc_sem,
+    az_sem, ax_sem, s_sem, sv_sem, hz_sem, hy_sem, hc_sem,
     b1_sem, b2_sem, b3_sem, c1_sem, c2_sem, c3_sem, dx_sem, dz_sem,
 ):
     dp, tp = lax.axis_index("dp"), lax.axis_index("tensor")
@@ -107,18 +107,27 @@
     to_x(0, h)
 
     arrived(peer_s, s_sem.at[0])
-    own, peer = gelu_parts(own_s[core]), gelu_parts(peer_s[...])
-    n = own[0].shape[0]
+    step, deep = rows.shape[2], b3_own.shape[1]
+    per = step // deep
+    shift = lax.rem(nz // 2 - 1 - per * h_far + nz, nz)
+    middle = [nz // 2 - 1 + i for i in range(per)]
+    outside = [i for i in range(nz) if i not in middle]
+
+    def piece_of(z_):
+        return lax.rem(z_ + nz - shift, nz)
+
+    own, peer = own_s[core].astype(f32), peer_s[...].astype(f32)
+    n = own.shape[0]
     first = core == 0
-    for ref, i in ((quad, 0), (slope, 1)):
-        ref[0:n, :] = jnp.where(first, own[i], peer[i])
-        ref[n : 2 * n, :] = jnp.where(first, peer[i], own[i])
-    hid[core, y, z] = quad[...].astype(bf16)
-
-    def to_z(buf, group, sem):
-        block = buf.at[core, y, z]
-        for k in range(1, nz):
-            send(block, block, group, sem.at[0], z_peer[k])
+    quad[0:n, :] = jnp.where(first, own, peer)
+    quad[n : 2 * n, :] = jnp.where(first, peer, own)
+    saved_send[...] = quad[...].astype(bf16)
+    send(saved_send, saved_recv, 14, sv_sem.at[0], at(z=lax.rem(z + shift, nz)))
+    hid[core, y, z] = gelu_parts(quad[...])[0].astype(bf16)
+
+    def to_z(block, group, sem):
+        for k in sorted(range(1, nz), key=lambda k: abs(2 * k - nz)):
+            send(block, block, group, sem, z_peer[k])
 
     def from_z(buf, sem):
         arrived(buf.at[core, y, 0 : nz - 1], sem.at[0])
@@ -129,7 +138,7 @@
     to_x(1, h_left)
     arrived(rows.at[slot(x, h_right)], az_sem.at[1])
     to_x(2, h_right)
-    near, step = nh - 1, rows.shape[2]
+    near = nh - 1
     groups = (h, h_left, h_right, h_far)
 
     def product(lo, hi):
@@ -173,43 +182,54 @@
     fold(0, near)
     arrived(rows.at[slot(x, h_far)], az_sem.at[2])
     to_x(near, h_far)
+    to_z(hid.at[core, y, z], 5, hz_sem.at[0])
     arrived(rows.at[0 : nx - 1], ax_sem.at[1])
     product(near, nh)
     fold(near, nh)
-    to_z(hid, 5, hz_sem)
-    for lo, hi in ((0, near), (near, nh)):
+    for lo, hi, owners in ((0, near, outside), (near, nh, middle)):
         arrived(b2_recv.at[:, lo:hi], b2_sem.at[1 if lo else 0])
         for g in range(lo, hi):
             total = b2_sum[g]
             for k in range(1, ny):
                 total = total + b2_recv[k - 1, g].astype(f32)
-            b2_rows[pl.ds(pl.multiple_of(groups[g] * step, step), step), :] = total
-    deep = b3_own.shape[1]
-    for j in range(nz):
-        piece = b2_rows[j * deep : (j + 1) * deep, :]
-        b3_own[j] = piece
-        b3_send[j] = piece.astype(bf16)
-    for k in range(1, nz):
-        send(b3_send.at[lax.rem(z + k, nz)], b3_recv.at[k - 1], 4, b3_sem.at[0], z_peer[k])
+            b2_sum[g] = total
+            for i in range(per):
+                piece = b2_sum[g, i * deep : (i + 1) * deep, :]
+                b3_own[groups[g] * per + i] = piece
+                b3_send[groups[g] * per + i] = piece.astype(bf16)
+        for owner in owners:
+
+            @pl.when(z != owner)
+            def _():
+                send(b3_send.at[piece_of(owner)], b3_recv.at[z], 4, b3_sem.at[0], at(z=owner))
+    mine = piece_of(z)
+    arrived(saved_recv, sv_sem.at[0])
+    slope[...] = gelu_parts(saved_recv[...])[1]
     from_z(hid, hz_sem)
     for k in range(1, ny):
         send(hid.at[core, y], hid.at[core, y], 7, hy_sem.at[0], y_peer[k])
-    total = b3_own[z]
-    arrived(b3_recv, b3_sem.at[0])
+    total = b3_own[mine]
+    arrived(b3_recv.at[0 : nz - 1], b3_sem.at[0])
     for k in range(1, nz):
-        total = total + b3_recv[k - 1].astype(f32)
-    pre[core, y, z] = (total * slope[...]).astype(bf16)
+        total = total + b3_recv[lax.rem(z + k, nz)].astype(f32)
+    pre[core, y, mine] = (total * slope[...]).astype(bf16)
     def gathered(which, out):
         for t in range(rows.shape[0]):
             wide[t * step : (t + 1) * step, :] = rows[t, which].astype(f32)
         out[...] = wide[...].astype(bf16)
 
-    to_z(pre, 6, c1_sem)
+    to_z(pre.at[core, y, mine], 6, c1_sem.at[z])
     gathered(0, grad_rows)
     gathered(1, input_rows)
-    from_z(pre, c1_sem)
-    per = step // deep
-    far_first = (near,) + tuple(range(near))
+
+    def from_owners(owners):
+        for owner in owners:
+
+            @pl.when(z != owner)
+            def _():
+                arrived(pre.at[core, y, piece_of(owner)], c1_sem.at[owner])
+
+    from_owners(middle)
 
     def part_of(half_, y_, g):
         return pre.at[half_, y_, pl.ds(groups[g] * per, per)]
@@ -217,11 +237,15 @@
     def y_back(k):
         return lax.rem(y + ny - k, ny)
 
-    for g in far_first:
+    def to_y(g):
         block = part_of(core, y, g)
         for k in range(1, ny):
             send(block, block, 9, c2_sem.at[k - 1 if g == near else ny - 1], y_peer[k])
         send(block, block, 10, c3_sem.at[0 if g == near else 1], partner)
+
+    to_y(near)
+    arrived(hid.at[core, 0 : ny - 1], hy_sem.at[0])
+    send(hid.at[core], hid.at[core], 8, hc_sem.at[0], partner)
 
     def packed(buf, which, out):
         for i in range(ny):
@@ -244,6 +268,9 @@
         block = part_of(core, y_back(k), near)
         arrived(block, c2_sem.at[k - 1])
         send(block, block, 10, c3_sem.at[0], partner)
+    from_owners(outside)
+    for g in range(near):
+        to_y(g)
     loaded(wi_v, 4)
     part = far_back(core)
     arrived(pre.at[other, :, 0:per], c3_sem.at[0])
@@ -253,19 +280,17 @@
     for k in range(1, nx):
         fx_send[k - 1] = fx_part[lax.rem(x + k, nx)].astype(bf16)
         send(fx_send.at[k - 1], fx_recv.at[k - 1], 11, dx_sem.at[1], x_peer[k])
-    arrived(pre.at[core, 0 : ny - 1, 0 : near * per], c2_sem.at[ny - 1])
-    for g in range(near):
-        for k in range(1, ny):
-            block = part_of(core, y_back(k), g)
-            send(block, block, 10, c3_sem.at[1], partner)
-    arrived(hid.at[core, 0 : ny - 1], hy_sem.at[0])
-    send(hid.at[core], hid.at[core], 8, hc_sem.at[0], partner)
     total = fx_part[x]
     arrived(fx_recv, dx_sem.at[1])
     for k in range(1, nx):
         total = total + fx_recv[k - 1].astype(f32)
     dz_send[0] = total.astype(bf16)
     send(dz_send.at[0], dz_recv.at[0], 13, dz_sem.at[0], right)
+    arrived(pre.at[core, 0 : ny - 1, 0 : near * per], c2_sem.at[ny - 1])
+    for g in range(near):
+        for k in range(1, ny):
+            block = part_of(core, y_back(k), g)
+            send(block, block, 10, c3_sem.at[1], partner)
     packed(pre, core, pre_full)
     part = back(pre_full[core], core)
     arrived(pre.at[other, :, 0 : near * per], c3_sem.at[1])
@@ -305,7 +330,7 @@
     sent = (
         rows.at[0 : 3 + nh * (nx - 1)], peer_s, b1_send, b2_send, b3_send.at[0 : nz - 1],
         hid.at[core, y, 0 : nz - 1], pre.at[core, y, 0 : nz - 1], hid.at[core, 0 : ny - 1],
-        hid.at[core], pre.at[core, 0 : ny - 1], pre.at[core], fx_send, dx_send, dz_send,
+        hid.at[core], pre.at[core, 0 : ny - 1], pre.at[core], fx_send, dx_send, dz_send, saved_send,
     )
     for group, ref in enumerate(sent):
         handle(ref, group, s_sem.at[0]).wait_send()
@@ -327,7 +352,6 @@
     half = hidden // 2
     tokens = step * nx * nh
     deep = tokens // (ny * nz)
-    per_y = tokens // ny
     vmem, dma = pltpu.VMEM, pltpu.SemaphoreType.DMA
     shapes = ((step, width), (width, hidden), (width, hidden))
     any_space = pl.BlockSpec(memory_space=pl.ANY)
@@ -347,6 +371,8 @@
             vmem((tokens, width), bf16),
             vmem((deep, half), f32),
             vmem((deep, half), f32),
+            vmem((deep, half), bf16),
+            vmem((deep, half), bf16),
             vmem((2, ny, nz, deep, half), bf16),
             vmem((2, ny, nz, deep, half), bf16),
             vmem((ny, nh, step, half), bf16),
@@ -355,10 +381,9 @@
             vmem((ny - 1, nh, step, half), bf16),
             vmem((ny - 1, nh, step, half), bf16),
             vmem((nh, step, half), f32),
-            vmem((per_y, half), f32),
             vmem((nz, deep, half), bf16),
             vmem((nz, deep, half), f32),
-            vmem((nz - 1, deep, half), bf16),
+            vmem((nz, deep, half), bf16),
             vmem((tokens, half), f32),
             vmem((2, tokens, half), bf16),
             vmem((2, tokens, half), bf16),
@@ -372,17 +397,18 @@
             vmem((3, step, width), bf16),
             vmem((3, step, width), bf16),
             dma((5,)),
-            dma((14,)),
+            dma((15,)),
             dma((3,)),
             dma((2,)),
             dma((1,)),
             dma((1,)),
             dma((1,)),
             dma((1,)),
+            dma((1,)),
             dma((ny + 1,)),
             dma((2,)),
             dma((1,)),
-            dma((1,)),
+            dma((nz,)),
             dma((ny,)),
             dma((2,)),
             dma((2,)),

time: 82.7 us -> 81 us (0.979)
  Pallas kernels: 82 us -> 80.2 us
    pallas_call x1, Pallas kernels: 80.9 us -> 79.1 us  [on_device(): pl.pallas_call(functools.partial(kernel, ny, nz, nx, nh), out_shape=tuple...]
where the time goes in v4:
time: 81 us; the launch traced here: 80.8 us
  Pallas kernels  80.2 us (99%)
    pallas_call x1, Pallas kernels, on_device(): pl.pallas_call(functools.partial(kernel, ny, nz, nx, nh), out_shape=tuple...  79.1 us

profile of v4, /device:TPU:1, one launch (start us, length us, event | category | flops | bytes accessed | tf_op | source)
XLA Modules:
  0.0 80.8 jit_solution(17871858704080655148)
XLA Ops:
  0.6 79.1 %shard_map.76 = (bf16[8,144]{1,0:T(8,128)(2,1)S(1)}, bf16[144,2304]{1,0:T(8,128)(2,1)S(1)}, bf16[144,2304]{1,0:T(8,128)(2,1)S(1)}) custom-call(bf16[8,144]{1,0:T(8,128)(2,1)} %x_hbm.1, bf16[8,144]{1,0:T(8,128)(2,1)} %g_hbm.1, bf16[2,2304]{1,0:T(2,128)(2,1)} %s_hbm.1, bf16[144,2304]{1,0:T(8,128)(2,1)} %wi_hbm.1, bf16[144,2304]{1,0:T(8,128)(2,1)} %bitcast.2), custom_call_target="tpu_custom_call" | custom-call | tf_op jit(solution)/shard_map/pallas_call | solution.py:358
  79.7 1.1 %shard_map.77 = (bf16[8,144]{1,0:T(8,128)(2,1)}, bf16[144,2304]{1,0:T(8,128)(2,1)}, bf16[144,2304]{1,0:T(8,128)(2,1)}) custom-call(bf16[8,144]{1,0:T(8,128)(2,1)S(1)} %get-tuple-element.9.refs_0_, bf16[144,2304]{1,0:T(8,128)(2,1)S(1)} %get-tuple-element.10.refs_1_, bf16[144,2304]{1,0:T(8,128)(2,1)S(1)} %get-tuple-element.11.refs_2_), custom_call_target="tpu_custom_call" | custom-call | tf_op jit(solution)/shard_map/pallas_call | solution.py:421

commit v5 on v4

--- a/solution.py
+++ b/solution.py
@@ -51,6 +51,9 @@
     partner = at(core=other)
     peers = y_peer[1:] + z_peer[1:] + x_peer[1:] + [right, left, partner]
 
+    def far_to_near(n):
+        return sorted(range(1, n), key=lambda k: -min(k, n - k))
+
     half = wi_v.shape[2]
 
     def load(src, dst, i):
@@ -93,7 +96,7 @@
 
     def to_x(which, h_):
         block = rows.at[slot(x, h_)]
-        for k in range(1, nx):
+        for k in far_to_near(nx):
             send(block, block, 0, ax_sem.at[0 if which < nh - 1 else 1], x_peer[k])
 
     load_g.wait()
@@ -126,7 +129,7 @@
     hid[core, y, z] = gelu_parts(quad[...])[0].astype(bf16)
 
     def to_z(block, group, sem):
-        for k in sorted(range(1, nz), key=lambda k: abs(2 * k - nz)):
+        for k in far_to_near(nz):
             send(block, block, group, sem, z_peer[k])
 
     def from_z(buf, sem):
@@ -175,7 +178,7 @@
             else:
                 b2_sum[lo:hi] = total
 
-    order = list(range(1, ny)) + [0]
+    order = far_to_near(ny) + [0]
     arrived(rows.at[0 : near * (nx - 1)], ax_sem.at[0])
     loaded(wo_v, 3)
     product(0, near)
@@ -239,7 +242,7 @@
 
     def to_y(g):
         block = part_of(core, y, g)
-        for k in range(1, ny):
+        for k in far_to_near(ny):
             send(block, block, 9, c2_sem.at[k - 1 if g == near else ny - 1], y_peer[k])
         send(block, block, 10, c3_sem.at[0 if g == near else 1], partner)
 
@@ -277,7 +280,7 @@
     part = part + far_back(other)
 
     fx_part[...] = part.reshape(fx_part.shape)
-    for k in range(1, nx):
+    for k in far_to_near(nx):
         fx_send[k - 1] = fx_part[lax.rem(x + k, nx)].astype(bf16)
         send(fx_send.at[k - 1], fx_recv.at[k - 1], 11, dx_sem.at[1], x_peer[k])
     total = fx_part[x]

time: 81 us -> 80.3 us (level)
  no operation moved by 1% of the time
where the time goes in v5:
time: 80.3 us; the launch traced here: 80.1 us
  Pallas kernels  79.5 us (99%)
    pallas_call x1, Pallas kernels, on_device(): pl.pallas_call(functools.partial(kernel, ny, nz, nx, nh), out_shape=tuple...  78.4 us

profile of v5, /device:TPU:1, one launch (start us, length us, event | category | flops | bytes accessed | tf_op | source)
XLA Modules:
  0.0 80.1 jit_solution(9570664890593356888)
XLA Ops:
  0.6 78.4 %shard_map.76 = (bf16[8,144]{1,0:T(8,128)(2,1)S(1)}, bf16[144,2304]{1,0:T(8,128)(2,1)S(1)}, bf16[144,2304]{1,0:T(8,128)(2,1)S(1)}) custom-call(bf16[8,144]{1,0:T(8,128)(2,1)} %x_hbm.1, bf16[8,144]{1,0:T(8,128)(2,1)} %g_hbm.1, bf16[2,2304]{1,0:T(2,128)(2,1)} %s_hbm.1, bf16[144,2304]{1,0:T(8,128)(2,1)} %wi_hbm.1, bf16[144,2304]{1,0:T(8,128)(2,1)} %bitcast.2), custom_call_target="tpu_custom_call" | custom-call | tf_op jit(solution)/shard_map/pallas_call | solution.py:361
  79.0 1.1 %shard_map.77 = (bf16[8,144]{1,0:T(8,128)(2,1)}, bf16[144,2304]{1,0:T(8,128)(2,1)}, bf16[144,2304]{1,0:T(8,128)(2,1)}) custom-call(bf16[8,144]{1,0:T(8,128)(2,1)S(1)} %get-tuple-element.9.refs_0_, bf16[144,2304]{1,0:T(8,128)(2,1)S(1)} %get-tuple-element.10.refs_1_, bf16[144,2304]{1,0:T(8,128)(2,1)S(1)} %get-tuple-element.11.refs_2_), custom_call_target="tpu_custom_call" | custom-call | tf_op jit(solution)/shard_map/pallas_call | solution.py:424

commit v6 on v5

--- a/solution.py
+++ b/solution.py
@@ -48,7 +48,7 @@
     z_peer = [None] + [at(z=lax.rem(z + k, nz)) for k in range(1, nz)]
     x_peer = [None] + [at(x=lax.rem(x + k, nx)) for k in range(1, nx)]
     right, left = at(h=lax.rem(h + 1, nh)), at(h=lax.rem(h + nh - 1, nh))
-    partner = at(core=other)
+    partner, opposite = at(core=other), at(h=lax.rem(h + 2, nh))
     peers = y_peer[1:] + z_peer[1:] + x_peer[1:] + [right, left, partner]
 
     def far_to_near(n):
@@ -288,7 +288,7 @@
     for k in range(1, nx):
         total = total + fx_recv[k - 1].astype(f32)
     dz_send[0] = total.astype(bf16)
-    send(dz_send.at[0], dz_recv.at[0], 13, dz_sem.at[0], right)
+    send(dz_send.at[0], dz_recv.at[0], 13, dz_sem.at[0], opposite)
     arrived(pre.at[core, 0 : ny - 1, 0 : near * per], c2_sem.at[ny - 1])
     for g in range(near):
         for k in range(1, ny):
@@ -312,8 +312,7 @@
         dz_part[g] = total
     dz_send[1] = dz_part[1].astype(bf16)
     send(dz_send.at[1], dz_recv.at[1], 13, dz_sem.at[1], left)
-    arrived(dz_recv.at[0], dz_sem.at[0])
-    dz_send[2] = (dz_part[2] + dz_recv[0].astype(f32)).astype(bf16)
+    dz_send[2] = dz_part[2].astype(bf16)
     send(dz_send.at[2], dz_recv.at[2], 13, dz_sem.at[2], right)
 
     def outer(a, b):
@@ -329,7 +328,11 @@
         gwo_v[:, i * half : (i + 1) * half] = outer(grad_rows, hid_full[i])
     arrived(dz_recv.at[1], dz_sem.at[1])
     arrived(dz_recv.at[2], dz_sem.at[2])
-    gin_v[...] = (dz_part[0] + dz_recv[1].astype(f32) + dz_recv[2].astype(f32)).astype(bf16)
+    arrived(dz_recv.at[0], dz_sem.at[0])
+    total = dz_part[0]
+    for i in range(3):
+        total = total + dz_recv[i].astype(f32)
+    gin_v[...] = total.astype(bf16)
     sent = (
         rows.at[0 : 3 + nh * (nx - 1)], peer_s, b1_send, b2_send, b3_send.at[0 : nz - 1],
         hid.at[core, y, 0 : nz - 1], pre.at[core, y, 0 : nz - 1], hid.at[core, 0 : ny - 1],

time: 80.3 us -> 80.6 us (level)
  no operation moved by 1% of the time
where the time goes in v6:
time: 80.6 us; the launch traced here: 80.4 us
  Pallas kernels  79.8 us (99%)
    pallas_call x1, Pallas kernels, on_device(): pl.pallas_call(functools.partial(kernel, ny, nz, nx, nh), out_shape=tuple...  78.7 us

profile of v6, /device:TPU:1, one launch (start us, length us, event | category | flops | bytes accessed | tf_op | source)
XLA Modules:
  0.0 80.4 jit_solution(17319681121937179978)
XLA Ops:
  0.6 78.7 %shard_map.76 = (bf16[8,144]{1,0:T(8,128)(2,1)S(1)}, bf16[144,2304]{1,0:T(8,128)(2,1)S(1)}, bf16[144,2304]{1,0:T(8,128)(2,1)S(1)}) custom-call(bf16[8,144]{1,0:T(8,128)(2,1)} %x_hbm.1, bf16[8,144]{1,0:T(8,128)(2,1)} %g_hbm.1, bf16[2,2304]{1,0:T(2,128)(2,1)} %s_hbm.1, bf16[144,2304]{1,0:T(8,128)(2,1)} %wi_hbm.1, bf16[144,2304]{1,0:T(8,128)(2,1)} %bitcast.2), custom_call_target="tpu_custom_call" | custom-call | tf_op jit(solution)/shard_map/pallas_call | solution.py:364
  79.4 1.1 %shard_map.77 = (bf16[8,144]{1,0:T(8,128)(2,1)}, bf16[144,2304]{1,0:T(8,128)(2,1)}, bf16[144,2304]{1,0:T(8,128)(2,1)}) custom-call(bf16[8,144]{1,0:T(8,128)(2,1)S(1)} %get-tuple-element.9.refs_0_, bf16[144,2304]{1,0:T(8,128)(2,1)S(1)} %get-tuple-element.10.refs_1_, bf16[144,2304]{1,0:T(8,128)(2,1)S(1)} %get-tuple-element.11.refs_2_), custom_call_target="tpu_custom_call" | custom-call | tf_op jit(solution)/shard_map/pallas_call | solution.py:427
